TPU v7x, 32 devices: a whole 2x2x4 slice. The times are simulated.
32 devices in a mesh: replica: 2 (over x), shard: 4 (over z), seq: 4 (over y, core).
Axes of the slice: x: 2, y: 2, z: 4, core: 2. Of those that a mesh axis runs over, the one named last changes fastest.
Arguments:
- tokens: bfloat16 [16, 1024, 768], P(('replica', 'shard'), 'seq'), may hold values from -6 to 6
- teacher: bfloat16 [16, 1024, 768], P(('replica', 'shard'), 'seq'), may hold values from -6 to 6
- seg_ids: int32 [16, 1024], P(('replica', 'shard'), 'seq'), may hold values from 0 to 7, never falling along the last dimension, each value on 1 to 512 neighbouring positions
- parent_seg: int32 [16, 8], P(('replica', 'shard')), may hold values from 0 to 6, as said below
- valid: int32 [16, 1024], P(('replica', 'shard'), 'seq'), may hold values from 0 to 1, as said below
- query_weight: bfloat16 [768, 768], P('shard'), may hold values from -0.21875 to 0.21875
- query_bias: bfloat16 [768], P('shard'), may hold values from -1.5 to 1.5
- key_weight: bfloat16 [768, 768], P('shard'), may hold values from -0.21875 to 0.21875
- value_weight: bfloat16 [768, 768], P('shard'), may hold values from -0.21875 to 0.21875
- value_bias: bfloat16 [768], P('shard'), may hold values from -1.5 to 1.5
- mix_weight: bfloat16 [768, 768], P('shard'), may hold values from -3.5 to 3.5
- mix_bias: bfloat16 [768], P('shard'), may hold values from -1.5 to 1.5
- first_gain: bfloat16 [768], P('shard'), may hold values from 0.5 to 1.5
- first_shift: bfloat16 [768], P('shard'), may hold values from -1.5 to 1.5
- inner_weight: bfloat16 [768, 3072], P('shard'), may hold values from -0.21875 to 0.21875
- inner_bias: bfloat16 [3072], P('shard'), may hold values from -1.5 to 1.5
- outer_weight: bfloat16 [3072, 768], P('shard'), may hold values from -0.109375 to 0.109375
- outer_bias: bfloat16 [768], P('shard'), may hold values from -1.5 to 1.5
- second_gain: bfloat16 [768], P('shard'), may hold values from 0.5 to 1.5
- second_shift: bfloat16 [768], P('shard'), may hold values from -1.5 to 1.5
Outputs:
- layer_out: bfloat16 [16, 1024, 768], P(('replica', 'shard'), 'seq')
- loss_value: float32 [], replicated
- input_grad: float32 [16, 1024, 768], P(('replica', 'shard'), 'seq')
- dquery_weight: float32 [768, 768], P('shard')
- dquery_bias: float32 [768], P('shard')
- dkey_weight: float32 [768, 768], P('shard')
- dvalue_weight: float32 [768, 768], P('shard')
- dvalue_bias: float32 [768], P('shard')
- dmix_weight: float32 [768, 768], P('shard')
- dmix_bias: float32 [768], P('shard')
- dfirst_gain: float32 [768], P('shard')
- dfirst_shift: float32 [768], P('shard')
- dinner_weight: float32 [768, 3072], P('shard')
- dinner_bias: float32 [3072], P('shard')
- douter_weight: float32 [3072, 768], P('shard')
- douter_bias: float32 [768], P('shard')
- dsecond_gain: float32 [768], P('shard')
- dsecond_shift: float32 [768], P('shard')
Inputs may be any that keep to these rules, and one draw needn't show every extreme that they name: `seg_ids`: in each tree the segment numbers never fall along the tokens, every one of the 8 segments has 1 to 512 tokens and one has exactly 512. parent_seg[t, 0] = 0 and parent_seg[t, s] < s for s >= 1, so segment 0 is an ancestor of every segment. valid[t, 0] = 1 in every tree.
All inputs are finite; a program needn't handle non-finite values.
Results may differ from a plain program's by a relative error of at most 0.014.
Values may be sent and summed in bfloat16 or wider, within the bound.
A program may use at most 192 MiB of HBM per device.

v0:
```python
import jax
import jax.numpy as jnp
from jax import lax
from jax.sharding import PartitionSpec as P

HEADS = 12
HD = 64
NSEG = 8


norm_eps = 1e-12


def layer_norm(resid, gain, shift):
    center = resid - jnp.mean(resid, axis=-1, keepdims=True)
    spread = jnp.mean(center * center, axis=-1, keepdims=True)
    return center * lax.rsqrt(spread + norm_eps) * gain + shift


def exact_gelu(values):
    return jax.nn.gelu(values, approximate=False)


def outer_sum(left, right):
    return lax.dot_general(
        left, right, (((0,), (0,)), ((), ())), preferred_element_type=jnp.float32
    )


def back_mul(grad, weight):
    return lax.dot_general(
        grad, weight, (((1,), (1,)), ((), ())), preferred_element_type=jnp.float32
    )


def forward_mul(left, right):
    return jnp.dot(left, right, preferred_element_type=jnp.float32)


def head_scores(query_head, key_head, allowed):
    scores = (
        jnp.einsum("tqd,tkd->tqk", query_head, key_head, preferred_element_type=jnp.float32) * 0.125
    )
    return jnp.where(allowed, scores, -1e30)


def split_heads(array, trees, length):
    return array.reshape(trees, length, HEADS, HD).transpose(2, 0, 1, 3)


def join_heads(array, trees, length):
    return array.transpose(1, 2, 0, 3).reshape(trees, length, HEADS * HD)


def per_device(
    tokens,
    teacher,
    seg_ids,
    parent_seg,
    valid,
    query_weight,
    query_bias,
    key_weight,
    value_weight,
    value_bias,
    mix_weight,
    mix_bias,
    first_gain,
    first_shift,
    inner_weight,
    inner_bias,
    outer_weight,
    outer_bias,
    second_gain,
    second_shift,
):
    trees, local_len, width = tokens.shape
    full_len = local_len * lax.axis_size("seq")
    row_count = trees * local_len
    total_slots = (
        row_count * lax.axis_size("replica") * lax.axis_size("shard") * lax.axis_size("seq")
    )
    valid_rows = valid.astype(jnp.float32)
    count = lax.psum(jnp.sum(valid_rows), ("replica", "shard", "seq"))
    gathered = (
        lax.all_gather(query_weight, "shard", axis=0, tiled=True),
        lax.all_gather(query_bias, "shard", axis=0, tiled=True),
        lax.all_gather(key_weight, "shard", axis=0, tiled=True),
        lax.all_gather(value_weight, "shard", axis=0, tiled=True),
        lax.all_gather(value_bias, "shard", axis=0, tiled=True),
        lax.all_gather(mix_weight, "shard", axis=0, tiled=True),
        lax.all_gather(mix_bias, "shard", axis=0, tiled=True),
        lax.all_gather(first_gain, "shard", axis=0, tiled=True),
        lax.all_gather(first_shift, "shard", axis=0, tiled=True),
        lax.all_gather(inner_weight, "shard", axis=0, tiled=True),
        lax.all_gather(inner_bias, "shard", axis=0, tiled=True),
        lax.all_gather(outer_weight, "shard", axis=0, tiled=True),
        lax.all_gather(outer_bias, "shard", axis=0, tiled=True),
        lax.all_gather(second_gain, "shard", axis=0, tiled=True),
        lax.all_gather(second_shift, "shard", axis=0, tiled=True),
    )
    (
        w_query,
        b_query,
        w_key,
        w_value,
        b_value,
        w_mix,
        b_mix,
        g_first,
        s_first,
        w_inner,
        b_inner,
        w_outer,
        b_outer,
        g_second,
        s_second,
    ) = gathered
    inputs = tokens.reshape(row_count, width)
    query = (forward_mul(inputs, w_query) + b_query.astype(jnp.float32)).astype(jnp.bfloat16)
    key_rows = forward_mul(inputs, w_key).astype(jnp.bfloat16)
    value_rows = (forward_mul(inputs, w_value) + b_value.astype(jnp.float32)).astype(jnp.bfloat16)
    tags = jnp.where(valid == 1, seg_ids, -1).astype(jnp.bfloat16)
    keys_all, values_all, tags_all = (
        lax.all_gather(key_rows.reshape(trees, local_len, width), "seq", axis=1, tiled=True),
        lax.all_gather(value_rows.reshape(trees, local_len, width), "seq", axis=1, tiled=True),
        lax.all_gather(tags, "seq", axis=1, tiled=True),
    )
    segment_range = jnp.arange(NSEG, dtype=jnp.int32)
    choose = (parent_seg[..., None] == segment_range).astype(jnp.float32)
    current = jnp.broadcast_to(jnp.eye(NSEG, dtype=jnp.float32), choose.shape)
    table = current
    for level in range(NSEG - 1):
        current = jnp.einsum("gsa,gab->gsb", current, choose, precision=lax.Precision.HIGHEST)
        table = jnp.maximum(table, current)
    query_onehot = (seg_ids[..., None] == segment_range).astype(jnp.float32)
    query_side = jnp.einsum("tqs,tsk->tqk", query_onehot, table, precision=lax.Precision.HIGHEST)
    key_side = (
        tags_all.astype(jnp.float32)[..., None] == jnp.arange(NSEG, dtype=jnp.float32)
    ).astype(jnp.float32)
    allowed = (
        jnp.einsum("tqs,tks->tqk", query_side, key_side, precision=lax.Precision.HIGHEST) > 0.5
    )
    query_heads = split_heads(query, trees, local_len)
    key_heads = split_heads(keys_all, trees, full_len)
    value_heads = split_heads(values_all, trees, full_len)

    def head_forward(head_items):
        query_head, key_head, value_head = head_items
        masked = head_scores(query_head, key_head, allowed)
        peak = jnp.max(masked, axis=-1, keepdims=True)
        expo = jnp.exp(masked - peak)
        total = jnp.sum(expo, axis=-1, keepdims=True)
        weights = (expo / total).astype(jnp.bfloat16)
        result = jnp.einsum("tqk,tkd->tqd", weights, value_head, preferred_element_type=jnp.float32)
        return (result, (peak + jnp.log(total))[..., 0])

    out_heads, log_total = lax.map(head_forward, (query_heads, key_heads, value_heads))
    attended = (
        join_heads(out_heads, trees, local_len).reshape(row_count, width).astype(jnp.bfloat16)
    )
    branch = forward_mul(attended, w_mix) + b_mix.astype(jnp.float32)
    resid_one = inputs.astype(jnp.float32) + branch
    first = layer_norm(resid_one, g_first.astype(jnp.float32), s_first.astype(jnp.float32))
    first_low = first.astype(jnp.bfloat16)
    hidden_pre = forward_mul(first_low, w_inner) + b_inner.astype(jnp.float32)
    hidden = exact_gelu(hidden_pre).astype(jnp.bfloat16)
    ffn = forward_mul(hidden, w_outer) + b_outer.astype(jnp.float32)
    resid_two = first + ffn
    output = layer_norm(resid_two, g_second.astype(jnp.float32), s_second.astype(jnp.float32))
    layer_out = output.astype(jnp.bfloat16).reshape(trees, local_len, width)
    error = output - teacher.reshape(row_count, width).astype(jnp.float32)
    row_weight = valid_rows.reshape(row_count, 1)
    local_loss = jnp.sum(row_weight * error * error)
    scale = total_slots / count
    grad_out = 2.0 * scale * row_weight * error
    w_query, w_key, w_value, w_mix, w_inner, w_outer, g_first, g_second = (
        lax.all_gather(query_weight, "shard", axis=0, tiled=True),
        lax.all_gather(key_weight, "shard", axis=0, tiled=True),
        lax.all_gather(value_weight, "shard", axis=0, tiled=True),
        lax.all_gather(mix_weight, "shard", axis=0, tiled=True),
        lax.all_gather(inner_weight, "shard", axis=0, tiled=True),
        lax.all_gather(outer_weight, "shard", axis=0, tiled=True),
        lax.all_gather(first_gain, "shard", axis=0, tiled=True),
        lax.all_gather(second_gain, "shard", axis=0, tiled=True),
    )
    second_pair = jax.vjp(
        layer_norm, resid_two, g_second.astype(jnp.float32), s_second.astype(jnp.float32)
    )
    grad_two, dsecond_gain, dsecond_shift = second_pair[1](grad_out)
    grad_ffn = grad_two.astype(jnp.bfloat16)
    douter_bias = jnp.sum(grad_ffn, axis=0, dtype=jnp.float32)
    douter_weight = outer_sum(hidden, grad_ffn)
    grad_hidden = back_mul(grad_ffn, w_outer)
    gelu_pair = jax.vjp(exact_gelu, hidden_pre)
    grad_pre = gelu_pair[1](grad_hidden)[0].astype(jnp.bfloat16)
    dinner_bias = jnp.sum(grad_pre, axis=0, dtype=jnp.float32)
    dinner_weight = outer_sum(first_low, grad_pre)
    grad_first = grad_two + back_mul(grad_pre, w_inner)
    first_pair = jax.vjp(
        layer_norm, resid_one, g_first.astype(jnp.float32), s_first.astype(jnp.float32)
    )
    grad_one, dfirst_gain, dfirst_shift = first_pair[1](grad_first)
    grad_branch = grad_one.astype(jnp.bfloat16)
    dmix_bias = jnp.sum(grad_branch, axis=0, dtype=jnp.float32)
    dmix_weight = outer_sum(attended, grad_branch)
    grad_attended = back_mul(grad_branch, w_mix).astype(jnp.bfloat16)
    grad_heads = split_heads(grad_attended, trees, local_len)

    def head_backward(head_items):
        query_head, key_head, value_head, grad_head, head_total = head_items
        masked = head_scores(query_head, key_head, allowed)
        probs = jnp.exp(masked - head_total[..., None])
        rounded = probs.astype(jnp.bfloat16)
        grad_value = jnp.einsum(
            "tqk,tqd->tkd", rounded, grad_head, preferred_element_type=jnp.float32
        )
        grad_probs = jnp.einsum(
            "tqd,tkd->tqk", grad_head, value_head, preferred_element_type=jnp.float32
        )
        inner = jnp.sum(probs * grad_probs, axis=-1, keepdims=True)
        grad_scores = (probs * (grad_probs - inner)).astype(jnp.bfloat16)
        grad_query = (
            jnp.einsum("tqk,tkd->tqd", grad_scores, key_head, preferred_element_type=jnp.float32)
            * 0.125
        )
        grad_key = (
            jnp.einsum("tqk,tqd->tkd", grad_scores, query_head, preferred_element_type=jnp.float32)
            * 0.125
        )
        return (grad_query, grad_key, grad_value)

    query_grads, key_grads, value_grads = lax.map(
        head_backward, (query_heads, key_heads, value_heads, grad_heads, log_total)
    )
    key_full = join_heads(key_grads, trees, full_len)
    value_full = join_heads(value_grads, trees, full_len)
    key_local, value_local = (
        lax.psum_scatter(key_full, "seq", scatter_dimension=1, tiled=True),
        lax.psum_scatter(value_full, "seq", scatter_dimension=1, tiled=True),
    )
    grad_query = (
        join_heads(query_grads, trees, local_len).reshape(row_count, width).astype(jnp.bfloat16)
    )
    grad_key = key_local.reshape(row_count, width).astype(jnp.bfloat16)
    grad_value = value_local.reshape(row_count, width).astype(jnp.bfloat16)
    dquery_weight = outer_sum(inputs, grad_query)
    dquery_bias = jnp.sum(grad_query, axis=0, dtype=jnp.float32)
    dkey_weight = outer_sum(inputs, grad_key)
    dvalue_weight = outer_sum(inputs, grad_value)
    dvalue_bias = jnp.sum(grad_value, axis=0, dtype=jnp.float32)
    input_grad = (
        grad_one
        + back_mul(grad_query, w_query)
        + back_mul(grad_key, w_key)
        + back_mul(grad_value, w_value)
    )
    owned = (
        lax.psum_scatter(dquery_weight, "shard", scatter_dimension=0, tiled=True),
        lax.psum_scatter(dquery_bias, "shard", scatter_dimension=0, tiled=True),
        lax.psum_scatter(dkey_weight, "shard", scatter_dimension=0, tiled=True),
        lax.psum_scatter(dvalue_weight, "shard", scatter_dimension=0, tiled=True),
        lax.psum_scatter(dvalue_bias, "shard", scatter_dimension=0, tiled=True),
        lax.psum_scatter(dmix_weight, "shard", scatter_dimension=0, tiled=True),
        lax.psum_scatter(dmix_bias, "shard", scatter_dimension=0, tiled=True),
        lax.psum_scatter(dfirst_gain, "shard", scatter_dimension=0, tiled=True),
        lax.psum_scatter(dfirst_shift, "shard", scatter_dimension=0, tiled=True),
        lax.psum_scatter(dinner_weight, "shard", scatter_dimension=0, tiled=True),
        lax.psum_scatter(dinner_bias, "shard", scatter_dimension=0, tiled=True),
        lax.psum_scatter(douter_weight, "shard", scatter_dimension=0, tiled=True),
        lax.psum_scatter(douter_bias, "shard", scatter_dimension=0, tiled=True),
        lax.psum_scatter(dsecond_gain, "shard", scatter_dimension=0, tiled=True),
        lax.psum_scatter(dsecond_shift, "shard", scatter_dimension=0, tiled=True),
    )
    summed = lax.psum(
        (
            owned[0],
            owned[1],
            owned[2],
            owned[3],
            owned[4],
            owned[5],
            owned[6],
            owned[7],
            owned[8],
            owned[9],
            owned[10],
            owned[11],
            owned[12],
            owned[13],
            owned[14],
        ),
        ("replica", "seq"),
    )
    loss_value = lax.psum(local_loss, ("replica", "shard", "seq")) / count
    return (
        layer_out,
        loss_value,
        input_grad.reshape(trees, local_len, width),
        summed[0],
        summed[1],
        summed[2],
        summed[3],
        summed[4],
        summed[5],
        summed[6],
        summed[7],
        summed[8],
        summed[9],
        summed[10],
        summed[11],
        summed[12],
        summed[13],
        summed[14],
    )


def solution(mesh):
    placed = (
        P(("replica", "shard"), "seq", None),
        P(("replica", "shard"), "seq", None),
        P(("replica", "shard"), "seq"),
        P(("replica", "shard"), None),
        P(("replica", "shard"), "seq"),
        P("shard", None),
        P("shard"),
        P("shard", None),
        P("shard", None),
        P("shard"),
        P("shard", None),
        P("shard"),
        P("shard"),
        P("shard"),
        P("shard", None),
        P("shard"),
        P("shard", None),
        P("shard"),
        P("shard"),
        P("shard"),
    )
    return jax.shard_map(
        per_device,
        mesh=mesh,
        in_specs=placed,
        out_specs=(
            P(("replica", "shard"), "seq", None),
            P(),
            P(("replica", "shard"), "seq", None),
            P("shard", None),
            P("shard"),
            P("shard", None),
            P("shard", None),
            P("shard"),
            P("shard", None),
            P("shard"),
            P("shard"),
            P("shard"),
            P("shard", None),
            P("shard"),
            P("shard", None),
            P("shard"),
            P("shard"),
            P("shard"),
        ),
        check_vma=False,
    )
```

profile of v0, /device:TPU:0, one launch (start us, length us, event | category | flops | bytes accessed | tf_op | source)
XLA Modules:
  0.0 1309.1 jit_solution(1301503991728295256)
XLA Ops:
  18.1 21.0 %all-reduce.20 = (bf16[768]{0:T(1024)(128)(2,1)S(1)}, bf16[768]{0:T(1024)(128)(2,1)S(1)}, bf16[768]{0:T(1024)(128)(2,1)S(1)}, bf16[768]{0:T(1024)(128)(2,1)S(1)}...) all-reduce(bf16[768]{0:T(1024)(128)(2,1)S(1)} %dynamic-update-slice, ...), channel_id=1, replica_groups=mesh['replica'=2,'shard'=4,'seq'=4] {'shard'}, use_global_device_ids=true, to_apply=%add | all-reduce | flops 6144 | bytes 24576
  39.2 4.1 all-gather.16.cloned.1.call-done
  43.2 2.3 add_convert_fusion.1
  46.8 27.7 %all-gather.12.cloned.1.call-done = bf16[768,768]{1,0:T(8,128)(2,1)} async-done(((bf16[192,768]{1,0:T(8,128)(2,1)}), bf16[768,768]{1,0:T(8,128)(2,1)}) %all-gather.12.cloned.1.call-update) | async-done | bytes 1179664 | tf_op jit(solution)/shard_map/all_gather | solution.py:88
  74.5 2.0 convolution_convert_fusion.1
  82.1 5.1 all_gather.66
  87.2 13.3 %all-gather = bf16[4,1,768]{2,1,0:T(2,128)(2,1)S(1)} all-gather(bf16[1,1,768]{2,1,0:T(2,128)(2,1)S(1)} %reshape.225), channel_id=1, replica_groups=mesh['replica'=2,'shard'=4,'seq'=4] {'shard'}, dimensions={0}, use_global_device_ids=true | all-gather | bytes 7680 | tf_op jit(solution)/shard_map/all_gather | solution.py:96
  100.5 38.8 %psum.120 = f32[]{:T(128)} all-reduce(f32[]{:T(128)} %convert_reduce_fusion.5), channel_id=1, replica_groups=mesh['replica'=2,'shard'=4,'seq'=4] {'replica','shard','seq'}, use_global_device_ids=true, to_apply=%region_11.12 | all-reduce | flops 1 | bytes 8 | tf_op jit(solution)/shard_map/psum | solution.py:84
  141.2 2.0 add_convert_fusion.2
  143.9 4.3 copy.69
  148.2 18.9 %all-gather.14.cloned.1.call-done = bf16[2,1024,768]{1,2,0:T(8,128)(2,1)} async-done(((bf16[2,256,768]{1,2,0:T(8,128)(2,1)}), bf16[2,1024,768]{1,2,0:T(8,128)(2,1)}) %all-gather.14.cloned.1.call-update) | async-done | bytes 3145744 | tf_op jit(solution)/shard_map/all_gather | solution.py:125
  167.0 4.0 copy.68
  171.2 44.5 %while.26 = (s32[]{:T(128)}, bf16[12,2,256,64]{2,3,1,0:T(8,128)(2,1)S(1)}, f32[12,2,256]{2,1,0:T(2,128)S(1)}, bf16[12,2,256,64]{2,3,1,0:T(8,128)(2,1)S(1)}, bf16...) while((s32[]{:T(128)}, ...), condition=%wide.region_3.4_spmd, body=%wide.region_0.3_spmd.sunk | while | flops 138411520 | bytes 7555161 | solution.py:158
  216.7 2.5 fusion.71
  220.6 68.4 %all-gather.22.cloned.1.call-done = bf16[768,3072]{1,0:T(8,128)(2,1)} async-done(((bf16[192,3072]{1,0:T(8,128)(2,1)}), bf16[768,3072]{1,0:T(8,128)(2,1)}) %all-gather.22.cloned.1.call-update) | async-done | bytes 4718608 | tf_op jit(solution)/shard_map/all_gather | solution.py:95
  289.1 21.1 %multiply_convert_fusion.1 = (bf16[512,3072]{1,0:T(8,128)(2,1)}, f32[512,3072]{1,0:T(8,128)}, f32[512,3072]{1,0:T(8,128)}) fusion(f32[3072]{0:T(1024)S(1)} %bitcast.240, bf16[768,3072]{1,0:T(8,128)(2,1)} %all-gather.22.cloned.1.call-done, f32[512,768]{1,0:T(8,128)} %copy-done.6, f32[768]{0:T(1024)S(1)} %convert_element_type.161, ...), kind=kOutput, calls=%fused_computation.50 | convolution fusion | flops 2521694208 | bytes 22042624 | tf_op jit(solution)/shard_map/dot_general | solution.py:37
  310.2 68.4 %all-gather.24.cloned.1.call-done = bf16[3072,768]{1,0:T(8,128)(2,1)} async-done(((bf16[768,768]{1,0:T(8,128)(2,1)}), bf16[3072,768]{1,0:T(8,128)(2,1)}) %all-gather.24.cloned.1.call-update) | async-done | bytes 4718608 | tf_op jit(solution)/shard_map/all_gather | solution.py:97
  378.5 6.0 fusion.72
  390.2 8.3 convert_reduce_fusion
  398.5 3.2 multiply_reduce_fusion.2
  408.1 108.5 %while.27 = (s32[]{:T(128)}, bf16[12,2,256,64]{2,3,1,0:T(8,128)(2,1)S(1)}, f32[12,2,1024,64]{2,3,0,1:T(8,128)}, f32[12,2,1024,64]{2,3,0,1:T(8,128)}, bf16[12,2,2...) while((s32[]{:T(128)}, ...), condition=%wide.region_18.19_spmd, body=%wide.region_16.18_spmd.sunk | while | flops 340426240 | bytes 18626676 | solution.py:233
  413.1 1.9 fusion.149
  422.1 2.0 fusion.149
  428.9 1.9 multiply_reduce_fusion.9
  440.0 2.0 fusion.149
  449.0 2.0 fusion.149
  455.9 1.9 multiply_reduce_fusion.9
  458.1 2.0 fusion.149
  464.9 1.9 multiply_reduce_fusion.9
  467.1 2.0 fusion.149
  476.1 2.0 fusion.149
  485.1 2.0 fusion.149
  494.1 2.0 fusion.149
  503.1 2.0 fusion.149
  512.1 1.9 fusion.149
  519.2 2.3 convolution_bitcast_fusion.4
  521.5 3.1 copy.85
  524.7 48.9 %reduce-scatter.17.cloned.1.call-done = f32[2,256,768]{1,2,0:T(8,128)} async-done(((f32[2,1024,768]{1,2,0:T(8,128)}), f32[2,256,768]{1,2,0:T(8,128)}) %reduce-scatter.17.cloned.1.call-update) | async-done | bytes 1572880 | tf_op jit(solution)/shard_map/reduce_scatter | solution.py:240
  576.1 3.3 convolution_bitcast_fusion.2
  579.4 3.1 copy.89
  582.7 51.9 %reduce-scatter.15.cloned.1.call-done = f32[2,256,768]{1,2,0:T(8,128)} async-done(((f32[2,1024,768]{1,2,0:T(8,128)}), f32[2,256,768]{1,2,0:T(8,128)}) %reduce-scatter.15.cloned.1.call-update) | async-done | bytes 1572880 | tf_op jit(solution)/shard_map/reduce_scatter | solution.py:239
  637.0 3.3 convolution_bitcast_fusion.3
  640.3 3.1 copy.87
  643.4 3.6 fusion.75
  647.1 8.9 fusion.62
  656.2 8.4 fusion.76
  664.7 20.8 %reduce-scatter.25.cloned.1.call-done = f32[192,768]{1,0:T(8,128)} async-done(((f32[768,768]{1,0:T(8,128)}), f32[192,768]{1,0:T(8,128)}) %reduce-scatter.25.cloned.1.call-update) | async-done | bytes 589840
  685.5 2.2 copy.86
  687.7 47.5 %reduce-scatter.29.cloned.1.call-done = f32[192,768]{1,0:T(8,128)} async-done(((f32[768,768]{1,0:T(8,128)}), f32[192,768]{1,0:T(8,128)}) %reduce-scatter.29.cloned.1.call-update) | async-done | bytes 589840
  735.3 2.2 copy.90
  737.5 47.6 %reduce-scatter.27.cloned.1.call-done = f32[192,768]{1,0:T(8,128)} async-done(((f32[768,768]{1,0:T(8,128)}), f32[192,768]{1,0:T(8,128)}) %reduce-scatter.27.cloned.1.call-update) | async-done | bytes 589840
  785.1 2.2 copy.88
  787.4 48.1 %reduce-scatter.19.cloned.1.call-done = f32[192,768]{1,0:T(8,128)} async-done(((f32[768,768]{1,0:T(8,128)}), f32[192,768]{1,0:T(8,128)}) %reduce-scatter.19.cloned.1.call-update) | async-done | bytes 589840 | tf_op jit(solution)/shard_map/reduce_scatter | solution.py:264
  835.4 163.0 %reduce-scatter.21.cloned.1.call-done = f32[192,3072]{1,0:T(8,128)} async-done(((f32[768,3072]{1,0:T(8,128)}), f32[192,3072]{1,0:T(8,128)}) %reduce-scatter.21.cloned.1.call-update) | async-done | bytes 2359312 | tf_op jit(solution)/shard_map/reduce_scatter | solution.py:268
  998.5 164.4 %reduce-scatter.23.cloned.1.call-done = f32[768,768]{1,0:T(8,128)} async-done(((f32[3072,768]{1,0:T(8,128)}), f32[768,768]{1,0:T(8,128)}) %reduce-scatter.23.cloned.1.call-update) | async-done | bytes 2359312 | tf_op jit(solution)/shard_map/reduce_scatter | solution.py:270
  1164.1 42.1 %psum.119 = f32[]{:T(128)} all-reduce(f32[]{:T(128)} %get-tuple-element.208), channel_id=1, replica_groups=mesh['replica'=2,'shard'=4,'seq'=4] {'replica','shard','seq'}, use_global_device_ids=true, to_apply=%region_9.10 | all-reduce | flops 1 | bytes 8 | tf_op jit(solution)/shard_map/psum | solution.py:295
  1207.9 3.6 fusion.73
  1213.0 18.4 %all-reduce.19 = (f32[768]{0:T(1024)S(1)}, f32[768]{0:T(1024)S(1)}, f32[768]{0:T(1024)S(1)}, f32[768]{0:T(1024)S(1)}, f32[768]{0:T(1024)S(1)}, /*index=5*/f32[30...) all-reduce(f32[768]{0:T(1024)S(1)} %reduce_sum.206, ...), channel_id=5, replica_groups=mesh['replica'=2,'shard'=4,'seq'=4] {'shard'}, use_global_device_ids=true, to_apply=%region_24.25.clone | all-reduce | flops 9216 | bytes 73728
  1232.1 23.0 %all-reduce.17 = (f32[192]{0:T(256)}, f32[192]{0:T(256)}, f32[192]{0:T(256)}, f32[192]{0:T(256)}, f32[192]{0:T(256)}, /*index=5*/f32[768]{0:T(1024)}, f32[192]{0:T(256)}, f32[192]{0:T(256)}, f32[192]{0:T(256)}) all-reduce(f32[192]{0:T(256)S(1)} %dynamic-slice.9, ...), channel_id=1, replica_groups=mesh['replica'=2,'shard'=4,'seq'=4] {'replica','seq'}, use_global_device_ids=true, to_apply=%region_25.26 | all-reduce | flops 2304 | bytes 18432 | tf_op jit(solution)/shard_map/psum | solution.py:275
  1255.0 2.8 fusion.74
  1258.3 2.1 add_add_fusion.2
  1260.4 29.4 %all-reduce.23.cloned.1.call-done = (f32[192,768]{0,1:T(8,128)}, f32[192,768]{0,1:T(8,128)}, f32[192,768]{0,1:T(8,128)}, f32[192,768]{1,0:T(8,128)}, f32[192,3072]{1,0:T(8,128)}, /*index=5*/f32[768,768]{1,0:T(8,128)}) async-done(((f32[192,768]{0,1:T(8,128)}, f32[192,768]{0,1:T(8,128)}, f32[192,768]{0,1:T(8,128)}, f32[192,768]{1,0:T(8,128)}, f32[192,3072]{1,0:T(8,128)}, /*index=5*/f32[768,768]{1,0:T(8,128)}), ...) | async-done | bytes 7077904 | tf_op jit(solution)/shard_map/psum | solution.py:275
  1289.8 2.3 copy.81
  1292.0 2.3 copy.82
  (319 shorter events, 175.3 us)
Async XLA Ops:
  7.2 36.0 %all-gather.16.cloned.1.call-start = ((), (), s32[]{:S(2)}) async-start(), calls=%async_computation.11 | async-start | bytes 1474560 | tf_op jit(solution)/shard_map/all_gather | solution.py:89
  7.9 66.5 %all-gather.12.cloned.1.call-start = ((), (), s32[]{:S(2)}) async-start(), calls=%async_computation.9 | async-start | bytes 1474560 | tf_op jit(solution)/shard_map/all_gather | solution.py:88
  8.7 132.5 %all-gather.10.cloned.1.call-start = ((), (), s32[]{:S(2)}) async-start(), calls=%async_computation.8 | async-start | bytes 1474560 | tf_op jit(solution)/shard_map/all_gather | solution.py:86
  9.4 134.5 %all-gather.18.cloned.1.call-start = ((), (), s32[]{:S(2)}) async-start(), calls=%async_computation.12 | async-start | bytes 3932160 | tf_op jit(solution)/shard_map/all_gather | solution.py:126
  45.5 28.9 %copy-start.4 = (bf16[2,256,768]{2,1,0:T(8,128)(2,1)S(1)}, bf16[2,256,768]{2,1,0:T(8,128)(2,1)}, u32[]{:S(2)}) copy-start(bf16[2,256,768]{2,1,0:T(8,128)(2,1)} %param.24) | copy-start | bytes 2359300
  46.7 120.3 %all-gather.14.cloned.1.call-start = ((), (), s32[]{:S(2)}) async-start(), calls=%async_computation.10 | async-start | bytes 3932160 | tf_op jit(solution)/shard_map/all_gather | solution.py:125
  77.7 2.2 copy-start.23
  77.7 3.6 copy-start.20
  77.7 4.2 copy-start.21
  77.7 9.5 copy-start.22
  77.7 139.0 %all-gather.20.cloned.1.call-start = ((), (), s32[]{:S(2)}) async-start(), calls=%async_computation.13 | async-start | bytes 1474560 | tf_op jit(solution)/shard_map/all_gather | solution.py:91
  78.3 210.8 %all-gather.22.cloned.1.call-start = ((), (), s32[]{:S(2)}) async-start(), calls=%async_computation.14 | async-start | bytes 5898240 | tf_op jit(solution)/shard_map/all_gather | solution.py:95
  79.0 299.5 %all-gather.24.cloned.1.call-start = ((), (), s32[]{:S(2)}) async-start(), calls=%async_computation.15 | async-start | bytes 5898240 | tf_op jit(solution)/shard_map/all_gather | solution.py:97
  79.8 493.8 %reduce-scatter.17.cloned.1.call-start = ((), (), s32[]{:S(2)}) async-start(), calls=%async_computation.17 | async-start | bytes 7864320 | tf_op jit(solution)/shard_map/reduce_scatter | solution.py:240
  215.7 3.5 copy-start.9
  216.7 2.5 copy-start.10
  219.2 1.1 copy-start.6
  289.1 89.5 %copy-start.7 = (f32[512,768]{1,0:T(8,128)S(1)}, f32[512,768]{1,0:T(8,128)}, u32[]{:S(2)}) copy-start(f32[512,768]{1,0:T(8,128)} %copy-done.6) | copy-start | bytes 4718596
  384.6 1.1 copy-start.12
  387.5 2.6 copy-start.24
  389.4 9.0 slice-start
  389.6 8.8 copy-start.18
  390.2 8.3 slice-start.1
  398.4 3.2 copy-start.26
  398.5 3.2 copy-start.8
  402.3 1.6 copy-start.25
  402.5 0.9 copy-start.13
  516.6 117.9 %reduce-scatter.15.cloned.1.call-start = ((), (), s32[]{:S(2)}) async-start(), calls=%async_computation.16 | async-start | bytes 7864320 | tf_op jit(solution)/shard_map/reduce_scatter | solution.py:239
  517.2 168.3 %reduce-scatter.25.cloned.1.call-start = ((), (), s32[]{:S(2)}) async-start(), calls=%async_computation.21 | async-start | bytes 2949120
  517.3 1.9 copy-start.5
  518.3 0.9 copy-start.11
  524.6 210.6 %reduce-scatter.29.cloned.1.call-start = ((), (), s32[]{:S(2)}) async-start(), calls=%async_computation.23 | async-start | bytes 2949120
  575.2 0.9 copy-start
  582.6 202.5 %reduce-scatter.27.cloned.1.call-start = ((), (), s32[]{:S(2)}) async-start(), calls=%async_computation.22 | async-start | bytes 2949120
  636.1 0.9 copy-start.2
  643.4 192.1 %reduce-scatter.19.cloned.1.call-start = ((), (), s32[]{:S(2)}) async-start(), calls=%async_computation.18 | async-start | bytes 2949120 | tf_op jit(solution)/shard_map/reduce_scatter | solution.py:264
  647.0 351.4 %reduce-scatter.21.cloned.1.call-start = ((), (), s32[]{:S(2)}) async-start(), calls=%async_computation.19 | async-start | bytes 11796480 | tf_op jit(solution)/shard_map/reduce_scatter | solution.py:268
  656.0 506.8 %reduce-scatter.23.cloned.1.call-start = ((), (), s32[]{:S(2)}) async-start(), calls=%async_computation.20 | async-start | bytes 11796480 | tf_op jit(solution)/shard_map/reduce_scatter | solution.py:270
  664.7 625.1 %all-reduce.23.cloned.1.call-start = ((), (), s32[]{:S(2)}) async-start(), calls=%async_computation.24 | async-start | bytes 15335424 | tf_op jit(solution)/shard_map/psum | solution.py:275
  1206.4 5.1 copy-start.3
  1207.9 4.8 copy-start.1
  1255.0 2.9 copy-start.16
  1255.0 3.3 copy-start.17
  1289.8 4.6 copy-start.19
  1292.0 5.3 copy-start.15
  1297.4 2.5 copy-start.14
Sparse Core Ops, SparseCore 0:
  9.6 33.5 all-gather.15
  44.8 29.6 all-gather.11
  76.0 29.8 all-gather.9
  107.9 28.2 all-gather.17
  138.1 28.8 all-gather.13
  168.5 30.4 all-gather.19
  200.5 88.5 all-gather.21
  290.6 87.8 all-gather.23
  516.8 56.8 reduce-scatter.16
  576.2 58.3 reduce-scatter.14
  637.5 48.0 reduce-scatter.24
  687.7 47.5 reduce-scatter.28
  737.6 47.5 reduce-scatter.26
  787.9 47.5 reduce-scatter.18
  837.6 160.7 reduce-scatter.20
  1000.7 162.1 reduce-scatter.22
  1167.3 122.4 all-reduce.22
where the time goes:
time: 1320 us; the launch traced here: 1310 us
  waiting for transfers between devices  814 us (62%)
  matrix products  222 us (17%)
  blocking collectives  162 us (12%)
  local copies, waits for them, and re-layouts  71.3 us (5%)
  between operations  20 us (2%)
  other arithmetic  18.7 us (1%)
    reduce_scatter x1, waiting for transfers between devices, per_device(): lax.psum_scatter(douter_weight, 'shard', scatter_dimension=0, tiled=True)  164 us
    reduce_scatter x1, waiting for transfers between devices, per_device(): lax.psum_scatter(dinner_weight, 'shard', scatter_dimension=0, tiled=True)  163 us
    unnamed x20, waiting for transfers between devices  121 us
    all_gather x1, waiting for transfers between devices, per_device(): lax.all_gather(inner_weight, 'shard', axis=0, tiled=True)  68.4 us
    all_gather x1, waiting for transfers between devices, per_device(): lax.all_gather(outer_weight, 'shard', axis=0, tiled=True)  68.4 us
    reduce_scatter x1, waiting for transfers between devices, per_device(): lax.psum_scatter(key_full, 'seq', scatter_dimension=1, tiled=True)  51.9 us
    reduce_scatter x1, waiting for transfers between devices, per_device(): lax.psum_scatter(value_full, 'seq', scatter_dimension=1, tiled=True)  48.9 us
    reduce_scatter x1, waiting for transfers between devices, per_device(): lax.psum_scatter(dmix_weight, 'shard', scatter_dimension=0, tiled=True)  48.1 us
  transfers between devices with their start and end apart: 17, of which 14 were waited for; matrix products, arithmetic and copies ran while one was open for 12% of the time, Pallas kernels for 0%

commit v1 on v0

v1 whole, which is shorter than its diff:
```python
import functools

import jax
import jax.numpy as jnp
from jax import lax
from jax.experimental import pallas as pl
from jax.experimental.pallas import tpu as pltpu
from jax.sharding import PartitionSpec as P

HEADS = 12
HD = 64
NSEG = 8
MESH = pl.DeviceIdType.MESH
BIG = 1e30
norm_eps = 1e-12
f32 = jnp.float32
bf16 = jnp.bfloat16
VMEM_LIMIT = 60 * 1024 * 1024


class Place:
    def __init__(self, nz):
        self.nz = nz
        self.x = lax.axis_index("replica")
        self.z = lax.axis_index("shard")
        self.q = lax.axis_index("seq")
        self.y = self.q // 2
        self.c = self.q % 2
        x, z, y, c = self.x, self.z, self.y, self.c
        self.core = (x, z, 2 * y + 1 - c)
        self.ynb = (x, z, 2 * (1 - y) + c)
        self.xnb = (1 - x, z, self.q)
        self.right = (x, z + 1, self.q)
        self.left = (x, z - 1, self.q)

    def greet(self):
        bar = pltpu.get_barrier_semaphore()
        for peer in (self.core, self.ynb, self.xnb):
            pl.semaphore_signal(bar, inc=1, device_id=peer, device_id_type=MESH)

        @pl.when(self.z > 0)
        def _():
            pl.semaphore_signal(bar, inc=1, device_id=self.left, device_id_type=MESH)

        @pl.when(self.z < self.nz - 1)
        def _():
            pl.semaphore_signal(bar, inc=1, device_id=self.right, device_id_type=MESH)

        peers = 3 + (self.z > 0).astype(jnp.int32) + (self.z < self.nz - 1).astype(jnp.int32)
        pl.semaphore_wait(bar, peers)


def rcopy(src, dst, ssem, rsem, dev):
    return pltpu.make_async_remote_copy(
        src_ref=src, dst_ref=dst, send_sem=ssem, recv_sem=rsem, device_id=dev, device_id_type=MESH
    )


def both(a, b):
    return jnp.logical_and(a, b)


def gather_body(
    nz, x_ref, tag_ref, pay_ref, mix_ref, inn_ref, out_ref,
    xa, taga, paya, mixa, inna, outa,
    loc, xs, xr, zs, zr, ns, nr, cs, cr,
):
    p = Place(nz)
    z, c, y, q = p.z, p.c, p.y, p.q
    rz = mix_ref.shape[0]
    length = x_ref.shape[1]
    half = mix_ref.shape[1] // 2
    quarter = inn_ref.shape[1] // 4
    p.greet()

    def token_block(j):
        return xa.at[:, pl.ds(pl.multiple_of(j * length, length), length)]

    x_core = rcopy(x_ref, token_block(q), xs.at[0], xr.at[0], p.core)
    x_y = rcopy(x_ref, token_block(q), xs.at[1], xr.at[1], p.ynb)
    qy = 2 * (1 - y) + c
    x_on = rcopy(token_block(qy), token_block(qy), xs.at[2], xr.at[2], p.core)
    t_core = rcopy(tag_ref, taga.at[q], xs.at[3], xr.at[3], p.core)
    t_y = rcopy(tag_ref, taga.at[q], xs.at[4], xr.at[4], p.ynb)
    t_on = rcopy(taga.at[qy], taga.at[qy], xs.at[5], xr.at[5], p.core)
    for cp in (t_y, t_core, x_y, x_core):
        cp.start()

    def mix_piece(ref):
        return ref.at[:, pl.ds(pl.multiple_of(c * half, half), half)]

    def inn_piece(ref, yy):
        return ref.at[:, pl.ds(pl.multiple_of((c * 2 + yy) * quarter, quarter), quarter)]

    def out_piece(ref, xx):
        return ref.at[pl.ds(pl.multiple_of((c * 2 + xx) * rz, 8), rz)]

    own = (
        lambda: pay_ref,
        lambda: mix_piece(mix_ref),
        lambda: inn_piece(inn_ref, y),
        lambda: out_piece(out_ref, p.x),
    )
    there = (
        lambda b: paya.at[b],
        lambda b: mix_piece(mixa.at[b]),
        lambda b: inn_piece(inna.at[b], y),
        lambda b: out_piece(outa.at[b], p.x),
    )
    other = {
        2: lambda b: inn_piece(inna.at[b], 1 - y),
        3: lambda b: out_piece(outa.at[b], 1 - p.x),
    }
    side = {2: p.ynb, 3: p.xnb}

    def zcopy(k, way, s, b, first):
        src = own[k]() if first else there[k](b)
        dev = p.right if way == 0 else p.left
        return rcopy(src, there[k](b), zs.at[k, way, s], zr.at[k, way, s], dev)

    def send_when(way, s):
        if way == 0:
            return both(z >= s - 1, z < nz - 1), z - s + 1
        return both(z <= nz - s, z > 0), z + s - 1

    def recv_when(way, s):
        if way == 0:
            return z >= s, z - s
        return z <= nz - 1 - s, z + s

    def live(s):
        return both(s >= 1, s <= nz - 1)

    def start_wave(k, s):
        for way in (0, 1):
            cond, b = send_when(way, s)
            cond = both(cond, live(s))

            @pl.when(both(cond, s == 1))
            def _():
                zcopy(k, way, s, b, True).start()

            @pl.when(both(cond, s > 1))
            def _():
                zcopy(k, way, s, b, False).start()

    def side_copy(k, b):
        return rcopy(there[k](b), there[k](b), ns.at[k - 2, b], nr.at[k - 2, b], side[k])

    def core_copy(k, b, part):
        piece = there[k](b) if part == 0 else other[k](b)
        return rcopy(piece, piece, cs.at[k - 1, part, b], cr.at[k - 1, part, b], p.core)

    def each(k, s, fn):
        for way in (0, 1):
            cond, b = recv_when(way, s)

            @pl.when(both(cond, live(s)))
            def _():
                fn(k, way, b)

    def take(k, s):
        def got(k, way, b):
            zcopy(k, way, s, b, False).wait_recv()
            if k >= 2:
                side_copy(k, b).start()
            if k >= 1:
                core_copy(k, b, 0).start()

        each(k, s, got)

    def pass_on(k, s):
        def got(k, way, b):
            side_copy(k, b).wait_recv()
            core_copy(k, b, 1).start()

        each(k, s, got)

    start_wave(0, jnp.int32(1))
    locals_ = [
        pltpu.make_async_copy(x_ref, token_block(q), loc.at[0]),
        pltpu.make_async_copy(tag_ref, taga.at[q], loc.at[1]),
        pltpu.make_async_copy(pay_ref, paya.at[z], loc.at[2]),
        pltpu.make_async_copy(mix_ref, mixa.at[z], loc.at[3]),
        pltpu.make_async_copy(inn_ref, inna.at[z], loc.at[4]),
        pltpu.make_async_copy(out_ref, outa.at[z], loc.at[5]),
    ]
    for cp in locals_:
        cp.start()

    def wave(w, carry):
        for k in range(4):
            s = w - k

            @pl.when(w > 1)
            def _():
                start_wave(k, s)

        for k in range(4):
            take(k, w - k)
        for k in (2, 3):
            pass_on(k, w - k - 1)

        @pl.when(w == 2)
        def _():
            x_y.wait_recv()
            x_on.start()
            t_y.wait_recv()
            t_on.start()

        return carry

    lax.fori_loop(1, nz + 4, wave, 0)

    for cp in locals_:
        cp.wait()
    for cp in (x_core, x_on, t_core, t_on):
        cp.wait()
    x_y.wait_send()
    t_y.wait_send()

    def drain(s, carry):
        for k in range(4):
            for way in (0, 1):
                cond, b = send_when(way, s)

                @pl.when(cond)
                def _():
                    zcopy(k, way, s, b, False).wait_send()

            def done(k, way, b):
                if k >= 2:
                    side_copy(k, b).wait_send()
                    core_copy(k, b, 1).wait()
                if k >= 1:
                    core_copy(k, b, 0).wait()

            each(k, s, done)
        return carry

    lax.fori_loop(1, nz, drain, 0)


def gather(nz, x, tags, pay, mix, inn, out):
    trees, length, width = x.shape
    dma = pltpu.SemaphoreType.DMA
    anyspace = pl.BlockSpec(memory_space=pl.ANY)
    return pl.pallas_call(
        functools.partial(gather_body, nz),
        out_shape=(
            jax.ShapeDtypeStruct((trees, 4 * length, width), x.dtype),
            jax.ShapeDtypeStruct((4,) + tags.shape, tags.dtype),
            jax.ShapeDtypeStruct((nz,) + pay.shape, pay.dtype),
            jax.ShapeDtypeStruct((nz,) + mix.shape, mix.dtype),
            jax.ShapeDtypeStruct((nz,) + inn.shape, inn.dtype),
            jax.ShapeDtypeStruct((nz,) + out.shape, out.dtype),
        ),
        in_specs=[anyspace] * 6,
        out_specs=[anyspace] * 6,
        scratch_shapes=[
            dma((6,)), dma((6,)), dma((6,)),
            dma((4, 2, nz)), dma((4, 2, nz)),
            dma((2, nz)), dma((2, nz)),
            dma((3, 2, nz)), dma((3, 2, nz)),
        ],
        compiler_params=pltpu.CompilerParams(collective_id=1, has_side_effects=True),
        name="gather_all",
    )(x, tags, pay, mix, inn, out)


def swap_body(nz, to_heads, in_ref, out_ref, loc, ss, rs):
    p = Place(nz)
    q = p.q
    bar = pltpu.get_barrier_semaphore()
    for d in (1, 2, 3):
        pl.semaphore_signal(bar, inc=1, device_id=(p.x, p.z, (q + d) % 4), device_id_type=MESH)
    pl.semaphore_wait(bar, 3)

    def src(j):
        return in_ref.at[j] if to_heads else in_ref.at[:, j]

    def dst(j):
        return out_ref.at[:, j] if to_heads else out_ref.at[j]

    copies = []
    for d in (1, 2, 3):
        t = (q + d) % 4
        cp = rcopy(src(t), dst(q), ss.at[d - 1], rs.at[d - 1], (p.x, p.z, t))
        cp.start()
        copies.append(cp)
    own = pltpu.make_async_copy(src(q), dst(q), loc)
    own.start()
    for cp in copies:
        cp.wait()
    own.wait()


def swap(nz, block, to_heads, cid):
    a, b = (0, 1) if to_heads else (1, 0)
    shape = (block.shape[1], block.shape[0]) + block.shape[2:]
    dma = pltpu.SemaphoreType.DMA
    anyspace = pl.BlockSpec(memory_space=pl.ANY)
    return pl.pallas_call(
        functools.partial(swap_body, nz, to_heads),
        out_shape=jax.ShapeDtypeStruct(shape, block.dtype),
        in_specs=[anyspace],
        out_specs=anyspace,
        scratch_shapes=[dma, dma((3,)), dma((3,))],
        compiler_params=pltpu.CompilerParams(collective_id=cid, has_side_effects=True),
        name="swap_heads" if to_heads else "swap_tokens",
    )(block)


def dot_nt(a, b):
    return lax.dot_general(a, b, (((1,), (1,)), ((), ())), preferred_element_type=f32)


def dot_tn(a, b):
    return lax.dot_general(a, b, (((0,), (0,)), ((), ())), preferred_element_type=f32)


def dot_nn(a, b):
    return jnp.dot(a, b, preferred_element_type=f32)


QB = 256


def attend_body(x_ref, w_ref, b_ref, qm_ref, km_ref, qkv_ref, att_ref, lse_ref):
    n = w_ref.shape[1] // 3
    heads = n // HD
    length = x_ref.shape[1]
    qkv_ref[0] = (dot_nn(x_ref[0], w_ref[...]) + b_ref[...]).astype(bf16)
    for h in range(heads):
        keys = jnp.concatenate([qkv_ref[0, :, n + h * HD : n + (h + 1) * HD], km_ref[0]], axis=1)
        values = qkv_ref[0, :, 2 * n + h * HD : 2 * n + (h + 1) * HD]

        def block(i, carry):
            rows = pl.ds(pl.multiple_of(i * QB, QB), QB)
            queries = jnp.concatenate(
                [qkv_ref[0, rows, h * HD : (h + 1) * HD] * 0.125, qm_ref[0, rows]], axis=1
            )
            s = dot_nt(queries, keys)
            peak = jnp.max(s, axis=1, keepdims=True)
            e = jnp.exp(s - peak)
            total = jnp.sum(e, axis=1, keepdims=True)
            o = dot_nn(e.astype(bf16), values) / total
            att_ref[0, rows, h * HD : (h + 1) * HD] = o.astype(bf16)
            lse_ref[0, rows, h : h + 1] = peak + jnp.log(total)
            return carry

        lax.fori_loop(0, length // QB, block, 0)


def attend(x_all, w, b, qm, km):
    trees, length, width = x_all.shape
    n3 = w.shape[1]
    tree = lambda d: pl.BlockSpec((1, length, d), lambda t: (t, 0, 0))
    return pl.pallas_call(
        attend_body,
        grid=(trees,),
        out_shape=(
            jax.ShapeDtypeStruct((trees, length, n3), bf16),
            jax.ShapeDtypeStruct((trees, length, n3 // 3), bf16),
            jax.ShapeDtypeStruct((trees, length, 8), f32),
        ),
        in_specs=[
            tree(width),
            pl.BlockSpec((width, n3), lambda t: (0, 0)),
            pl.BlockSpec((1, n3), lambda t: (0, 0)),
            tree(HD),
            tree(HD),
        ],
        out_specs=[tree(n3), tree(n3 // 3), tree(8)],
        compiler_params=pltpu.CompilerParams(vmem_limit_bytes=VMEM_LIMIT),
        name="attend",
    )(x_all, w, b, qm, km)


def attend_back_body(qkv_ref, do_ref, lse_ref, qm_ref, km_ref, d_ref, dk_ref, dv_ref):
    n = qkv_ref.shape[2] // 3
    heads = n // HD
    length = qkv_ref.shape[1]
    for h in range(heads):
        cols = slice(h * HD, (h + 1) * HD)
        key = qkv_ref[0, :, n + h * HD : n + (h + 1) * HD]
        keys = jnp.concatenate([key, km_ref[0]], axis=1)
        values = qkv_ref[0, :, 2 * n + h * HD : 2 * n + (h + 1) * HD]
        dk_ref[...] = jnp.zeros_like(dk_ref)
        dv_ref[...] = jnp.zeros_like(dv_ref)

        def block(i, carry):
            rows = pl.ds(pl.multiple_of(i * QB, QB), QB)
            query = qkv_ref[0, rows, cols]
            queries = jnp.concatenate([query * 0.125, qm_ref[0, rows]], axis=1)
            s = dot_nt(queries, keys)
            probs = jnp.exp(s - lse_ref[0, rows, h : h + 1])
            grad = do_ref[0, rows, cols]
            dp = dot_nt(grad, values)
            inner = jnp.sum(probs * dp, axis=1, keepdims=True)
            ds = (probs * (dp - inner)).astype(bf16)
            dv_ref[...] += dot_tn(probs.astype(bf16), grad)
            dk_ref[...] += dot_tn(ds, query)
            d_ref[0, rows, cols] = (dot_nn(ds, key) * 0.125).astype(bf16)
            return carry

        lax.fori_loop(0, length // QB, block, 0)
        d_ref[0, :, n + h * HD : n + (h + 1) * HD] = (dk_ref[...] * 0.125).astype(bf16)
        d_ref[0, :, 2 * n + h * HD : 2 * n + (h + 1) * HD] = dv_ref[...].astype(bf16)


def attend_back(qkv, do, lse, qm, km):
    trees, length, n3 = qkv.shape
    tree = lambda d: pl.BlockSpec((1, length, d), lambda t: (t, 0, 0))
    return pl.pallas_call(
        attend_back_body,
        grid=(trees,),
        out_shape=jax.ShapeDtypeStruct((trees, length, n3), bf16),
        in_specs=[tree(n3), tree(n3 // 3), tree(8), tree(HD), tree(HD)],
        out_specs=tree(n3),
        scratch_shapes=[pltpu.VMEM((length, HD), f32), pltpu.VMEM((length, HD), f32)],
        compiler_params=pltpu.CompilerParams(vmem_limit_bytes=VMEM_LIMIT),
        name="attend_back",
    )(qkv, do, lse, qm, km)


def add_to(dst, src):
    dst[...] = (dst[...].astype(f32) + src[...].astype(f32)).astype(dst.dtype)


def reduce_body(
    nz, inn, out, mix, qkv, ig, vec,
    o_inn, o_out, o_mix, o_qkv, o_ig, o_vec,
    ci, co, cm, cg, xi, yo, yi, xo, yg, zi, zo, zm, zq, aq, xm, ym, xq, v_in, v_z, v_acc,
    loc, cs, cr, s1, r1, s2, r2, zs, zr, gs, gr, vs, vr,
):
    p = Place(nz)
    z, c, y, x, q = p.z, p.c, p.y, p.x, p.q
    rz = mix.shape[1]
    wide = inn.shape[2]
    width = mix.shape[2]
    h = width // 2
    p.greet()

    def lanes(start, size):
        return pl.ds(pl.multiple_of(start, 128), size)

    def rows(start, size):
        return pl.ds(pl.multiple_of(start, 8), size)

    w2, w4, w8 = wide // 2, wide // 4, wide // 8
    first = [
        rcopy(ig.at[:, 1 - c], cg.at[0], cs.at[0], cr.at[0], p.core),
        rcopy(ig.at[:, 3 - c], cg.at[1], cs.at[1], cr.at[1], p.core),
        rcopy(vec, v_in.at[0], cs.at[2], cr.at[2], p.core),
        rcopy(mix.at[:, :, lanes((1 - c) * h, h)], cm, cs.at[3], cr.at[3], p.core),
        rcopy(out.at[:, :, lanes((1 - c) * h, h)], co, cs.at[4], cr.at[4], p.core),
        rcopy(inn.at[:, :, lanes((1 - c) * w2, w2)], ci, cs.at[5], cr.at[5], p.core),
    ]
    for cp in first:
        cp.start()

    def ig_sum(b):
        @pl.when(c == 0)
        def _():
            add_to(cg.at[b], ig.at[:, 2 * b])

        @pl.when(c == 1)
        def _():
            add_to(cg.at[b], ig.at[:, 2 * b + 1])

    first[0].wait()
    first[1].wait()
    ig_sum(0)
    ig_sum(1)
    ig_y = rcopy(cg.at[1 - y], yg, s1.at[2], r1.at[2], p.ynb)
    ig_y.start()

    first[2].wait()
    v_acc[...] = vec[...] + v_in[0]
    v_x = rcopy(v_acc, v_in.at[1], vs.at[0], vr.at[0], p.xnb)
    v_x.start()

    first[3].wait()

    def mix_sum(i, carry):
        add_to(cm.at[i], mix.at[i, :, lanes(c * h, h)])
        return carry

    lax.fori_loop(0, nz, mix_sum, 0)

    first[4].wait()

    def out_sum(i, carry):
        for j in range(4):
            add_to(co.at[i, j * rz : (j + 1) * rz], out.at[i, j * rz : (j + 1) * rz, lanes(c * h, h)])
        return carry

    lax.fori_loop(0, nz, out_sum, 0)
    out_y = rcopy(co.at[:, rows((1 - y) * 2 * rz, 2 * rz)], yo, s1.at[1], r1.at[1], p.ynb)
    out_y.start()
    first[5].wait()

    def inn_sum(i, carry):
        for j in range(4):
            add_to(ci.at[i, :, j * w8 : (j + 1) * w8], inn.at[i, :, lanes(c * w2 + j * w8, w8)])
        return carry

    lax.fori_loop(0, nz, inn_sum, 0)
    inn_x = rcopy(ci.at[:, :, lanes((1 - x) * w4, w4)], xi, s1.at[0], r1.at[0], p.xnb)
    inn_x.start()

    def chain(k, acc, buf):
        def copy(way, s, d):
            dev = p.right if way == 0 else p.left
            return rcopy(acc(d), buf(way, d), zs.at[k, way, s], zr.at[k, way, s], dev)

        def sending(way, s):
            if way == 0:
                d = z + nz - s
                return both(d <= nz - 1, z < nz - 1), d
            d = z - nz + s
            return both(d >= 0, z > 0), d

        def getting(way, s):
            if way == 0:
                d = z - 1 + nz - s
                return both(d <= nz - 1, z > 0), d
            d = z + 1 - nz + s
            return both(d >= 0, z < nz - 1), d

        def send(s):
            for way in (0, 1):
                ok, d = sending(way, s)

                @pl.when(ok)
                def _():
                    copy(way, s, d).start()

        def get(s):
            for way in (0, 1):
                ok, d = getting(way, s)

                @pl.when(ok)
                def _():
                    copy(way, s, d).wait_recv()
                    add_to(acc(d), buf(way, d))

        def drain(s, carry):
            for way in (0, 1):
                ok, d = sending(way, s)

                @pl.when(ok)
                def _():
                    copy(way, s, d).wait_send()

            return carry

        return send, get, lambda: lax.fori_loop(1, nz, drain, 0)

    def own_qkv(i, carry):
        aq[i] = qkv[i]
        return carry

    lax.fori_loop(0, nz, own_qkv, 0)
    qkv_chain = chain(0, lambda d: aq.at[d], lambda way, d: zq.at[way, d])
    mix_chain = chain(1, lambda d: cm.at[d], lambda way, d: zm.at[way, d])

    def late(s, carry):
        qkv_chain[0](s)
        mix_chain[0](s)
        qkv_chain[1](s)
        mix_chain[1](s)
        return carry

    lax.fori_loop(1, nz, late, 0)

    v_x.wait()
    v_acc[...] = v_acc[...] + v_in[1]
    v_y = rcopy(v_acc, v_in.at[2], vs.at[1], vr.at[1], p.ynb)
    v_y.start()

    x_q = rcopy(aq.at[z], xq, gs.at[0], gr.at[0], p.xnb)
    x_m = rcopy(cm.at[z], xm, gs.at[1], gr.at[1], p.xnb)
    x_q.start()
    x_m.start()

    inn_x.wait()

    def inn_sum2(i, carry):
        add_to(xi.at[i], ci.at[i, :, lanes(x * w4, w4)])
        return carry

    lax.fori_loop(0, nz, inn_sum2, 0)
    inn_y = rcopy(xi.at[:, :, lanes((1 - y) * w8, w8)], yi, s2.at[0], r2.at[0], p.ynb)
    inn_y.start()
    out_y.wait()

    def out_sum2(i, carry):
        add_to(yo.at[i], co.at[i, rows(y * 2 * rz, 2 * rz)])
        return carry

    lax.fori_loop(0, nz, out_sum2, 0)
    out_x = rcopy(yo.at[:, rows((1 - x) * rz, rz)], xo, s2.at[1], r2.at[1], p.xnb)
    out_x.start()

    v_y.wait()
    v_acc[...] = v_acc[...] + v_in[2]
    v_z[z] = v_acc[...]

    ig_y.wait()
    o_ig[...] = (cg[y].astype(f32) + yg[...].astype(f32)).astype(o_ig.dtype)

    x_q.wait()
    o_qkv[q] = (aq[z].astype(f32) + xq[...].astype(f32)).astype(bf16)
    q_core = rcopy(o_qkv.at[q], o_qkv.at[q], gs.at[2], gr.at[2], p.core)
    q_y = rcopy(o_qkv.at[q], o_qkv.at[q], gs.at[3], gr.at[3], p.ynb)
    q_y.start()
    q_core.start()
    x_m.wait()
    add_to(xm, cm.at[z])
    y_m = rcopy(xm, ym, gs.at[4], gr.at[4], p.ynb)
    y_m.start()

    inn_y.wait()

    def inn_sum3(i, carry):
        add_to(yi.at[i], xi.at[i, :, lanes(y * w8, w8)])
        return carry

    lax.fori_loop(0, nz, inn_sum3, 0)
    out_x.wait()

    def out_sum3(i, carry):
        add_to(xo.at[i], yo.at[i, rows(x * rz, rz)])
        return carry

    lax.fori_loop(0, nz, out_sum3, 0)

    inn_chain = chain(2, lambda d: yi.at[d], lambda way, d: zi.at[way, d])
    out_chain = chain(3, lambda d: xo.at[d], lambda way, d: zo.at[way, d])

    def vcopy(way, s, b):
        dev = p.right if way == 0 else p.left
        return rcopy(v_z.at[b], v_z.at[b], zs.at[4, way, s], zr.at[4, way, s], dev)

    def vsend(way, s):
        if way == 0:
            return both(z >= s - 1, z < nz - 1), z - s + 1
        return both(z <= nz - s, z > 0), z + s - 1

    def vget(way, s):
        if way == 0:
            return z >= s, z - s
        return z <= nz - 1 - s, z + s

    def last(s, carry):
        inn_chain[0](s)
        out_chain[0](s)
        for way in (0, 1):
            ok, b = vsend(way, s)

            @pl.when(ok)
            def _():
                vcopy(way, s, b).start()

        inn_chain[1](s)
        out_chain[1](s)
        for way in (0, 1):
            ok, b = vget(way, s)

            @pl.when(ok)
            def _():
                vcopy(way, s, b).wait_recv()

        return carry

    lax.fori_loop(1, nz, last, 0)

    def i_at(xx, yy):
        return o_inn.at[:, lanes(c * w2 + xx * w4 + yy * w8, w8)]

    def i_half(xx):
        return o_inn.at[:, lanes(c * w2 + xx * w4, w4)]

    def o_at(xx, yy):
        return o_out.at[rows((2 * yy + xx) * rz, rz), lanes(c * h, h)]

    def o_half(yy):
        return o_out.at[rows(2 * yy * rz, 2 * rz), lanes(c * h, h)]

    o_inn[:, lanes(c * w2 + x * w4 + y * w8, w8)] = yi[z]
    o_out[rows((2 * y + x) * rz, rz), lanes(c * h, h)] = xo[z]
    i_y = rcopy(i_at(x, y), i_at(x, y), gs.at[5], gr.at[5], p.ynb)
    o_x = rcopy(o_at(x, y), o_at(x, y), gs.at[6], gr.at[6], p.xnb)
    i_y.start()
    o_x.start()
    y_m.wait()
    o_mix[:, lanes(c * h, h)] = (xm[...].astype(f32) + ym[...].astype(f32)).astype(bf16)
    m_core = rcopy(
        o_mix.at[:, lanes(c * h, h)], o_mix.at[:, lanes(c * h, h)], gs.at[7], gr.at[7], p.core
    )
    m_core.start()
    q_y.wait()
    qy = 2 * (1 - y) + c
    q_on = rcopy(o_qkv.at[qy], o_qkv.at[qy], gs.at[8], gr.at[8], p.core)
    q_on.start()

    def v_sum(i, carry):
        return carry + v_z[i]

    o_vec[...] = lax.fori_loop(0, nz, v_sum, jnp.zeros(o_vec.shape, f32))

    i_y.wait()
    i_x = rcopy(i_half(x), i_half(x), gs.at[9], gr.at[9], p.xnb)
    i_x.start()
    o_x.wait()
    o_y = rcopy(o_half(y), o_half(y), gs.at[10], gr.at[10], p.ynb)
    o_y.start()
    i_x.wait()
    i_all = o_inn.at[:, lanes(c * w2, w2)]
    i_core = rcopy(i_all, i_all, gs.at[11], gr.at[11], p.core)
    i_core.start()
    o_y.wait()
    o_all = o_out.at[:, lanes(c * h, h)]
    o_core = rcopy(o_all, o_all, gs.at[12], gr.at[12], p.core)
    o_core.start()
    for cp in (m_core, q_core, q_on, i_core, o_core):
        cp.wait()
    for ch in (qkv_chain, mix_chain, inn_chain, out_chain):
        ch[2]()

    def vdrain(s, carry):
        for way in (0, 1):
            ok, b = vsend(way, s)

            @pl.when(ok)
            def _():
                vcopy(way, s, b).wait_send()

        return carry

    lax.fori_loop(1, nz, vdrain, 0)


def reduce_all(nz, inn, out, mix, qkv, ig, vec):
    rz, width = mix.shape[1], mix.shape[2]
    wide = inn.shape[2]
    h, w2, w4, w8 = width // 2, wide // 2, wide // 4, wide // 8
    n3 = qkv.shape[2]
    trees, _, length, _ = ig.shape
    dma = pltpu.SemaphoreType.DMA
    V = pltpu.VMEM
    vm = pl.BlockSpec(memory_space=pltpu.VMEM)
    return pl.pallas_call(
        functools.partial(reduce_body, nz),
        out_shape=(
            jax.ShapeDtypeStruct((rz, wide), bf16),
            jax.ShapeDtypeStruct((4 * rz, width), bf16),
            jax.ShapeDtypeStruct((rz, width), bf16),
            jax.ShapeDtypeStruct((4, rz, n3), bf16),
            jax.ShapeDtypeStruct((trees, length, width), bf16),
            jax.ShapeDtypeStruct(vec.shape, f32),
        ),
        in_specs=[vm] * 6,
        out_specs=[vm] * 6,
        scratch_shapes=[
            V((nz, rz, w2), bf16),
            V((nz, 4 * rz, h), bf16),
            V((nz, rz, h), bf16),
            V((2, trees, length, width), bf16),
            V((nz, rz, w4), bf16),
            V((nz, 2 * rz, h), bf16),
            V((nz, rz, w8), bf16),
            V((nz, rz, h), bf16),
            V((trees, length, width), bf16),
            V((2, nz, rz, w8), bf16),
            V((2, nz, rz, h), bf16),
            V((2, nz, rz, h), bf16),
            V((2, nz, rz, n3), bf16),
            V((nz, rz, n3), bf16),
            V((rz, h), bf16),
            V((rz, h), bf16),
            V((rz, n3), bf16),
            V((3,) + vec.shape, f32),
            V((nz,) + vec.shape, f32),
            V(vec.shape, f32),
            dma,
            dma((6,)), dma((6,)),
            dma((3,)), dma((3,)),
            dma((2,)), dma((2,)),
            dma((5, 2, nz)), dma((5, 2, nz)),
            dma((13,)), dma((13,)),
            dma((2,)), dma((2,)),
        ],
        compiler_params=pltpu.CompilerParams(
            collective_id=4, has_side_effects=True, vmem_limit_bytes=VMEM_LIMIT
        ),
        name="reduce_all",
    )(inn, out, mix, qkv, ig, vec)


def normed(resid):
    center = resid - jnp.mean(resid, axis=-1, keepdims=True)
    spread = jnp.mean(center * center, axis=-1, keepdims=True)
    inv = lax.rsqrt(spread + norm_eps)
    return center * inv, inv


def norm_back(grad_hat, hat, inv):
    mean = jnp.mean(grad_hat, axis=-1, keepdims=True)
    along = jnp.mean(grad_hat * hat, axis=-1, keepdims=True)
    return inv * (grad_hat - mean - hat * along)


def per_device(
    nz,
    tokens, teacher, seg_ids, parent_seg, valid,
    query_weight, query_bias, key_weight, value_weight, value_bias,
    mix_weight, mix_bias, first_gain, first_shift,
    inner_weight, inner_bias, outer_weight, outer_bias, second_gain, second_shift,
):
    trees, local_len, width = tokens.shape
    n_seq = lax.axis_size("seq")
    full_len = local_len * n_seq
    row_count = trees * local_len
    total_slots = row_count * lax.axis_size("replica") * nz * n_seq
    seq = lax.axis_index("seq")
    rz = mix_weight.shape[0]
    cols = width // n_seq

    def mine(w):
        return lax.dynamic_slice_in_dim(w, seq * cols, cols, axis=1)

    heads_weight = jnp.concatenate([mine(query_weight), mine(key_weight), mine(value_weight)], axis=1)
    small = (query_bias, value_bias, mix_bias, first_gain, first_shift, outer_bias, second_gain, second_shift, inner_bias)
    flat = jnp.concatenate(small)
    flat = jnp.pad(flat, (0, 8 * 3 * cols - flat.shape[0])).reshape(8, 3 * cols)
    pay = jnp.concatenate([heads_weight, flat], axis=0)
    tags = jnp.where(valid == 1, seg_ids, seg_ids + NSEG).reshape(1, row_count)
    tags = jnp.broadcast_to(tags, (8, row_count))

    x_all, tags_all, pay_all, mix_all, inn_all, out_all = gather(
        nz, tokens, tags, pay, mix_weight, inner_weight, outer_weight
    )

    vecs = pay_all[:, rz:].reshape(nz, -1)
    whole = [vecs[:, i * rz : (i + 1) * rz].reshape(width).astype(f32) for i in range(8)]
    b_query, b_value, b_mix, g_first, s_first, b_outer, g_second, s_second = whole
    b_inner = vecs[:, 8 * rz : 8 * rz + inner_bias.shape[0]].reshape(-1).astype(f32)
    w_heads = pay_all[:, :rz].reshape(width, 3 * cols)
    w_mix = mix_all.reshape(width, width)
    w_inner = inn_all.reshape(width, -1)
    w_outer = out_all.reshape(-1, width)

    def own_part(v):
        return lax.dynamic_slice_in_dim(v, seq * cols, cols, axis=0)

    b_heads = jnp.concatenate([own_part(b_query), jnp.zeros((cols,), f32), own_part(b_value)])[None]

    segment_range = jnp.arange(NSEG, dtype=jnp.int32)
    choose = (parent_seg[..., None] == segment_range).astype(f32)
    current = jnp.broadcast_to(jnp.eye(NSEG, dtype=f32), choose.shape)
    table = current
    for level in range(NSEG - 1):
        current = jnp.sum(current[..., None] * choose[:, None], axis=2)
        table = jnp.maximum(table, current)
    tag = tags_all[:, 0].reshape(n_seq, trees, local_len).transpose(1, 0, 2).reshape(trees, full_len)
    segs = tag % NSEG
    hidden_key = (tag >= NSEG).astype(f32)
    onehot = (segs[..., None] == segment_range).astype(f32)
    seen = jnp.sum(onehot[..., None] * table[:, None], axis=2)
    q_feat = jnp.concatenate(
        [(seen - 1.0) * BIG, jnp.full((trees, full_len, 1), -BIG, f32)], axis=-1
    )
    k_feat = jnp.concatenate([onehot, hidden_key[..., None]], axis=-1)
    pad = ((0, 0), (0, 0), (0, HD - NSEG - 1))
    q_feat = jnp.pad(q_feat, pad).astype(bf16)
    k_feat = jnp.pad(k_feat, pad).astype(bf16)

    qkv, att_heads, lse = attend(x_all, w_heads, b_heads, q_feat, k_feat)
    att_blocks = swap(nz, att_heads.reshape(trees, n_seq, local_len, cols), False, 2)
    attended = att_blocks.reshape(n_seq, row_count, cols).transpose(1, 0, 2).reshape(row_count, width)

    inputs = tokens.reshape(row_count, width)
    resid_one = inputs.astype(f32) + dot_nn(attended, w_mix) + b_mix
    hat_one, inv_one = normed(resid_one)
    first = hat_one * g_first + s_first
    first_low = first.astype(bf16)
    hidden_pre = dot_nn(first_low, w_inner) + b_inner
    cdf = 0.5 + 0.5 * lax.erf(hidden_pre * (0.5**0.5))
    slope = cdf + hidden_pre * jnp.exp(-0.5 * hidden_pre * hidden_pre) * 0.3989422804014327
    hidden = (hidden_pre * cdf).astype(bf16)
    resid_two = first + dot_nn(hidden, w_outer) + b_outer
    hat_two, inv_two = normed(resid_two)
    output = hat_two * g_second + s_second
    layer_out = output.astype(bf16).reshape(trees, local_len, width)
    error = output - teacher.reshape(row_count, width).astype(f32)
    row_weight = valid.astype(f32).reshape(row_count, 1)
    weighted = row_weight * error
    local_loss = jnp.sum(weighted * error)
    local_count = jnp.sum(row_weight)

    grad_out = 2.0 * weighted
    dsecond_gain = jnp.sum(grad_out * hat_two, axis=0)
    dsecond_shift = jnp.sum(grad_out, axis=0)
    grad_two = norm_back(grad_out * g_second, hat_two, inv_two)
    grad_ffn = grad_two.astype(bf16)
    douter_bias = jnp.sum(grad_ffn, axis=0, dtype=f32)
    douter_weight = dot_tn(hidden, grad_ffn).astype(bf16)
    grad_pre = (dot_nt(grad_ffn, w_outer) * slope).astype(bf16)
    dinner_bias = jnp.sum(grad_pre, axis=0, dtype=f32)
    dinner_weight = dot_tn(first_low, grad_pre).astype(bf16)
    grad_first = grad_two + dot_nt(grad_pre, w_inner)
    dfirst_gain = jnp.sum(grad_first * hat_one, axis=0)
    dfirst_shift = jnp.sum(grad_first, axis=0)
    grad_one = norm_back(grad_first * g_first, hat_one, inv_one)
    grad_branch = grad_one.astype(bf16)
    dmix_bias = jnp.sum(grad_branch, axis=0, dtype=f32)
    dmix_weight = dot_tn(attended, grad_branch).astype(bf16)
    grad_attended = dot_nt(grad_branch, w_mix).astype(bf16)
    grad_blocks = grad_attended.reshape(trees, local_len, n_seq, cols).transpose(2, 0, 1, 3)
    grad_heads = swap(nz, grad_blocks, True, 3).reshape(trees, full_len, cols)

    dqkv = attend_back(qkv, grad_heads, lse, q_feat, k_feat).reshape(trees * full_len, 3 * cols)
    dheads = dot_tn(x_all.reshape(trees * full_len, width), dqkv).astype(bf16)
    dbias = jnp.sum(dqkv, axis=0, dtype=f32)
    partial = dot_nt(dqkv, w_heads).astype(bf16).reshape(trees, n_seq, local_len, width)

    def place(v):
        return lax.dynamic_update_slice_in_dim(jnp.zeros((width,), f32), v, seq * cols, axis=0)

    scalars = jnp.concatenate([jnp.stack([local_loss, local_count]), jnp.zeros((width - 2,), f32)])
    vec = jnp.concatenate(
        [place(dbias[:cols]), place(dbias[2 * cols :]), dmix_bias, dfirst_gain, dfirst_shift,
         douter_bias, dsecond_gain, dsecond_shift, dinner_bias, scalars]
    ).reshape(-1, width)
    vec = jnp.pad(vec, ((0, 16 - vec.shape[0]), (0, 0)))

    r_inn, r_out, r_mix, r_qkv, r_ig, r_vec = reduce_all(
        nz,
        dinner_weight.reshape(nz, rz, -1),
        douter_weight.reshape(nz, 4 * rz, width),
        dmix_weight.reshape(nz, rz, width),
        dheads.reshape(nz, rz, 3 * cols),
        partial,
        vec,
    )
    flat = r_vec.reshape(-1)
    wide = inner_bias.shape[0] * nz
    spot = 8 * width + wide
    count = flat[spot + 1]
    scale = total_slots / count
    loss_value = flat[spot] / count
    shard = lax.axis_index("shard")

    def vec_out(i):
        return lax.dynamic_slice_in_dim(flat, i * width + shard * rz, rz, axis=0) * scale

    dinner_bias = (
        lax.dynamic_slice_in_dim(flat, 8 * width + shard * inner_bias.shape[0], inner_bias.shape[0], axis=0) * scale
    )

    def full(w):
        return w.astype(f32) * scale

    def heads_out(i):
        part = r_qkv[:, :, i * cols : (i + 1) * cols].transpose(1, 0, 2).reshape(rz, width)
        return full(part)

    input_grad = (grad_one.reshape(trees, local_len, width) + r_ig.astype(f32)) * scale
    return (
        layer_out, loss_value, input_grad,
        heads_out(0), vec_out(0), heads_out(1), heads_out(2), vec_out(1),
        full(r_mix), vec_out(2), vec_out(3), vec_out(4),
        full(r_inn), dinner_bias, full(r_out), vec_out(5), vec_out(6), vec_out(7),
    )


def solution(mesh):
    rows = P(("replica", "shard"), "seq", None)
    line = P(("replica", "shard"), "seq")
    mat = P("shard", None)
    row = P("shard")
    placed = (
        rows, rows, line, P(("replica", "shard"), None), line,
        mat, row, mat, mat, row, mat, row, row, row, mat, row, mat, row, row, row,
    )
    return jax.shard_map(
        functools.partial(per_device, mesh.shape["shard"]),
        mesh=mesh,
        in_specs=placed,
        out_specs=(
            rows, P(), rows,
            mat, row, mat, mat, row, mat, row, row, row, mat, row, mat, row, row, row,
        ),
        check_vma=False,
    )
```

time: 1320 us -> 438 us (0.33)
  waiting for transfers between devices: 814 us -> 0 us
  Pallas kernels: 0 us -> 315 us
  matrix products: 222 us -> 53 us
  blocking collectives: 162 us -> 0 us
  local copies, waits for them, and re-layouts: 71.3 us -> 34 us
  between operations: 20 us -> 4.77 us
    reduce_scatter x5 -> x0, waiting for transfers between devices: 476 us -> none  [the longest x1 164 us: per_device(): lax.psum_scatter(douter_weight, 'shard', scatter_dimension=0, tiled=True)]
    pallas_call x0 -> x6, Pallas kernels: none -> 315 us  [the longest x1 118 us: gather(): pl.pallas_call(functools.partial(gather_body, nz), out_shape=(jax.ShapeDt...]
    all_gather x8 -> x0, waiting for transfers between devices: 187 us -> none  [the longest x1 68.4 us: per_device(): lax.all_gather(inner_weight, 'shard', axis=0, tiled=True)]
    dot_general x111 -> x11, matrix products: 222 us -> 53 us  [the longest x4 18.2 us: dot_nt(): lax.dot_general(a, b, (((1,), (1,)), ((), ())), preferred_element_type=f32)]
    unnamed x20 -> x0, waiting for transfers between devices: 121 us -> none
    psum x3 -> x0, blocking collectives: 104 us -> none  [the longest x1 42.1 us: per_device(): loss_value = lax.psum(local_loss, ('replica', 'shard', 'seq')) / count]
    unnamed x100 -> x43, local copies, waits for them, and re-layouts: 43.5 us -> 0.84 us
    unnamed x2 -> x0, blocking collectives: 39.4 us -> none
  transfers between devices with their start and end apart: 17 -> 0, of which waited for: 14 -> 0; matrix products, arithmetic and copies ran while one was open for 12% -> 0% of each run, Pallas kernels for 0% -> 0%
where the time goes in v1:
time: 438 us; the launch traced here: 431 us
  Pallas kernels  315 us (72%)
  matrix products  53 us (12%)
  local copies, waits for them, and re-layouts  34 us (8%)
  other arithmetic  23.8 us (5%)
  between operations  4.77 us (1%)
    pallas_call x1, Pallas kernels, gather(): pl.pallas_call(functools.partial(gather_body, nz), out_shape=(jax.ShapeDt...  118 us
    pallas_call x1, Pallas kernels, reduce_all(): pl.pallas_call(functools.partial(reduce_body, nz), out_shape=(jax.ShapeDt...  111 us
    pallas_call x1, Pallas kernels, attend_back(): pl.pallas_call(attend_back_body, grid=(trees,), out_shape=jax.ShapeDtypeS...  33.6 us
    pallas_call x2, Pallas kernels, swap(): pl.pallas_call(functools.partial(swap_body, nz, to_heads), out_shape=jax....  27.7 us
    pallas_call x1, Pallas kernels, attend(): pl.pallas_call(attend_body, grid=(trees,), out_shape=(jax.ShapeDtypeStruc...  24.8 us
    dot_general x4, matrix products, dot_nt(): lax.dot_general(a, b, (((1,), (1,)), ((), ())), preferred_element_type=f32)  18.2 us
    dot_general x4, matrix products, dot_tn(): lax.dot_general(a, b, (((0,), (0,)), ((), ())), preferred_element_type=f32)  17.9 us
    dot_general x3, matrix products, dot_nn(): return jnp.dot(a, b, preferred_element_type=f32)  16.9 us

profile of v1, /device:TPU:0, one launch (start us, length us, event | category | flops | bytes accessed | tf_op | source)
XLA Modules:
  0.0 430.6 jit_solution(1160745882132048735)
XLA Ops:
  0.7 0.8 fusion.15
  1.5 0.1 multiply_reduce_fusion.14
  2.2 1.1 constant_dynamic-slice_fusion
  3.3 0.1 constant_dynamic-slice_fusion.2
  3.4 6.1 %concatenate.23 = bf16[2304]{0:T(1024)(128)(2,1)S(1)} concatenate(bf16[192]{0:T(256)(128)(2,1)} %param.26, bf16[192]{0:T(256)(128)(2,1)} %param.29, bf16[192]{0:T(256)(128)(2,1)} %param.31, bf16[192]{0:T(256)(128)(2,1)} %param.32, bf16[192]{0:T(256)(128)(2,1)} %param.33, bf16[192]{0:T(256)(128)(2,1)} %param.37, bf16[192]{0:T(256)(128)(2,1)} %param.38, bf16[192]{0:T(256)(128)(2,1)} %param.39, ...), dimensions={0} | concatenate | bytes 9216 | tf_op jit(solution)/shard_map/concatenate | solution.py:837
  9.7 0.8 pad_maximum_fusion.pay_ref
  10.5 0.8 convert_bitcast_fusion
  11.2 0.6 broadcast_in_dim.13.tag_ref
  11.8 118.0 %gather_all.1 = (bf16[2,1024,768]{2,1,0:T(8,128)(2,1)}, s32[4,8,512]{2,1,0:T(8,128)}, bf16[4,200,576]{2,1,0:T(8,128)(2,1)}, bf16[4,192,768]{2,1,0:T(8,128)(2,1)}...) custom-call(bf16[2,256,768]{2,1,0:T(8,128)(2,1)} %x_ref.1, s32[8,512]{1,0:T(8,128)} %broadcast_in_dim.13.tag_ref, ...), custom_call_target="tpu_custom_call" | custom-call | tf_op jit(solution)/shard_map/gather_all/pallas_call | solution.py:248
  129.9 1.0 slice_reduce_fusion
  131.0 0.1 multiply_reduce_fusion.7
  131.1 0.3 copy.79
  131.4 0.9 fusion.12.qm_ref
  132.3 0.1 reshape.306
  132.9 0.6 broadcast_in_dim.15.b_ref
  133.6 0.3 copy.80
  133.9 0.9 pad.21.km_ref
  134.8 1.1 slice.57
  135.8 24.8 %attend.1 = (bf16[2,1024,576]{2,1,0:T(8,128)(2,1)}, bf16[2,1024,192]{2,1,0:T(8,128)(2,1)}, f32[2,1024,8]{2,1,0:T(8,128)}) custom-call(bf16[2,1024,768]{2,1,0:T(8,128)(2,1)} %get-tuple-element.33.x_ref, bf16[768,576]{1,0:T(8,128)(2,1)} %bitcast.91, f32[1,576]{1,0:T(1,128)} %broadcast_in_dim.15.b_ref, bf16[2,1024,64]{2,1,0:T(8,128)(2,1)} %fusion.12.qm_ref, ...), custom_call_target="tpu_custom_call" | custom-call | tf_op jit(solution)/shard_map/attend/pallas_call | solution.py:359
  160.6 13.7 %swap_tokens.1 = bf16[4,2,256,192]{3,2,1,0:T(8,128)(2,1)} custom-call(bf16[2,4,256,192]{3,2,1,0:T(8,128)(2,1)} %bitcast.96), custom_call_target="tpu_custom_call" | custom-call | tf_op jit(solution)/shard_map/swap_tokens/pallas_call | solution.py:303
  174.3 1.5 copy.81
  175.9 2.4 fusion.27
  178.3 0.3 multiply_reduce_fusion.5
  178.8 8.5 %multiply_convert_fusion = (bf16[512,3072]{1,0:T(8,128)(2,1)}, f32[512,3072]{1,0:T(8,128)}) fusion(f32[3072]{0:T(1024)S(1)} %reshape.333, bf16[768,3072]{1,0:T(8,128)(2,1)} %bitcast.105, f32[512,768]{1,0:T(8,128)S(1)} %get-tuple-element.90, f32[768]{0:T(1024)S(1)} %reshape.332, f32[768]{0:T(1024)S(1)} %reshape.331, f32[512]{0:T(512)S(1)} %add_rsqrt_fusion.1, ...), kind=kOutput, calls=%fused_computation.8 | convolution fusion | flops 2427322368 | bytes 15751168 | tf_op jit(solution)/shard_map/dot_general | solution.py:323
  187.4 6.0 %fusion.28 = (f32[512]{0:T(512)S(1)}, f32[512,768]{1,0:T(8,128)S(1)}) fusion(f32[768]{0:T(1024)S(1)} %reshape.334, bf16[512,3072]{1,0:T(8,128)(2,1)} %get-tuple-element.91, bf16[3072,768]{1,0:T(8,128)(2,1)} %bitcast.109, f32[768]{0:T(1024)S(1)} %reshape.332, f32[768]{0:T(1024)S(1)} %reshape.331, f32[512]{0:T(512)S(1)} %add_rsqrt_fusion.1, ...), kind=kOutput, calls=%fused_computation.124 | convolution fusion | flops 2418671104 | bytes 11025408 | tf_op jit(solution)/shard_map/dot_general | solution.py:323
  193.4 0.3 multiply_reduce_fusion.4
  193.9 3.2 fusion.6
  197.1 1.7 convert_reduce_fusion.2
  198.9 6.8 %convert_reduce_fusion = (f32[3072]{0:T(1024)S(1)}, bf16[512,3072]{1,0:T(8,128)(2,1)S(1)}) fusion(f32[512,3072]{1,0:T(8,128)S(1)} %copy-done.15, f32[3072]{0:T(1024)S(1)} %reshape.333, bf16[3072,768]{1,0:T(8,128)(2,1)} %bitcast.110, f32[512,768]{1,0:T(8,128)S(1)} %get-tuple-element.60), kind=kOutput, calls=%fused_computation.7 | convolution fusion | flops 2436756480 | bytes 15753216 | tf_op jit(solution)/shard_map/dot_general | solution.py:315
  205.8 3.1 multiply_reduce_fusion.1
  208.9 0.5 convert_reduce_fusion.3
  209.5 0.7 copy-done.14
  210.2 1.8 convolution_convert_fusion.4
  212.0 3.6 reshape.341
  215.6 2.4 copy.96
  217.9 14.1 %swap_heads.1 = bf16[2,4,256,192]{3,2,1,0:T(8,128)(2,1)} custom-call(bf16[4,2,256,192]{3,2,1,0:T(8,128)(2,1)} %bitcast.89), custom_call_target="tpu_custom_call" | custom-call | tf_op jit(solution)/shard_map/swap_heads/pallas_call | solution.py:303
  232.0 33.6 %attend_back.1 = bf16[2,1024,576]{2,1,0:T(8,128)(2,1)} custom-call(bf16[2,1024,576]{2,1,0:T(8,128)(2,1)} %get-tuple-element.40.qkv_ref, bf16[2,1024,192]{2,1,0:T(8,128)(2,1)} %bitcast.90, f32[2,1024,8]{2,1,0:T(8,128)} %get-tuple-element.41.lse_ref, bf16[2,1024,64]{2,1,0:T(8,128)(2,1)} %fusion.12.qm_ref, bf16[2,1024,64]{2,1,0:T(8,128)(2,1)} %pad.21.km_ref), custom_call_target="tpu_custom_call" | custom-call | tf_op jit(solution)/shard_map/attend_back/pallas_call | solution.py:415
  265.6 2.3 convert_reduce_fusion.1
  267.8 0.1 slice_dynamic-update-slice_fusion
  268.0 0.6 convert_reduce_fusion.4
  268.7 1.4 concatenate.28
  270.0 0.6 pad.22.vec
  270.7 6.4 %convolution_convert_fusion.2 = bf16[2048,768]{1,0:T(8,128)(2,1)} fusion(bf16[2048,576]{1,0:T(8,128)(2,1)} %bitcast.84, bf16[768,576]{1,0:T(8,128)(2,1)} %bitcast.92), kind=kOutput, calls=%fused_computation.13 | convolution fusion | flops 1813512192 | bytes 6389760 | tf_op jit(solution)/shard_map/dot_general | solution.py:315
  277.1 3.1 bitcast_convert_fusion
  280.2 2.5 copy.85
  282.6 3.0 convolution_convert_fusion.3
  285.7 6.8 %convolution_convert_fusion = bf16[3072,768]{1,0:T(8,128)(2,1)} fusion(bf16[512,3072]{1,0:T(8,128)(2,1)} %get-tuple-element.91, f32[512,768]{1,0:T(8,128)S(1)} %copy-done.7), kind=kOutput, calls=%fused_computation.11 | convolution fusion | flops 2418671616 | bytes 9437184 | tf_op jit(solution)/shard_map/dot_general | solution.py:319
  292.5 4.9 %convolution_convert_fusion.1 = bf16[768,3072]{1,0:T(8,128)(2,1)} fusion(bf16[512,3072]{1,0:T(8,128)(2,1)S(1)} %copy-done.17, f32[512,768]{1,0:T(8,128)S(1)} %get-tuple-element.90, f32[768]{0:T(1024)S(1)} %reshape.332, f32[768]{0:T(1024)S(1)} %reshape.331, f32[512]{0:T(512)S(1)} %add_rsqrt_fusion.1, f32[512]{0:T(512)S(1)} %broadcast_multiply_fusion.6), kind=kOutput, calls=%fused_computation.12 | convolution fusion | flops 2420244480 | bytes 9447424 | tf_op jit(solution)/shard_map/dot_general | solution.py:319
  297.5 110.9 %reduce_all.1 = (bf16[192,3072]{1,0:T(8,128)(2,1)}, bf16[768,768]{1,0:T(8,128)(2,1)}, bf16[192,768]{1,0:T(8,128)(2,1)}, bf16[4,192,576]{2,1,0:T(8,128)(2,1)}, bf...) custom-call(bf16[4,192,3072]{2,1,0:T(8,128)(2,1)} %bitcast.87, bf16[4,768,768]{2,1,0:T(8,128)(2,1)} %bitcast.86, ...), custom_call_target="tpu_custom_call" | custom-call | tf_op jit(solution)/shard_map/reduce_all/pallas_call | solution.py:755
  408.4 0.8 reshape.324
  409.2 0.6 fusion.26
  410.5 2.9 convert_multiply_fusion
  413.4 0.7 dynamic-slice_multiply_fusion
  414.1 1.7 convert_multiply_fusion.1
  415.7 0.9 convert_multiply_fusion.2
  416.6 0.7 dynamic-slice_multiply_fusion.1
  417.3 2.4 multiply_bitcast_fusion
  419.7 0.5 copy.86
  420.2 1.3 mul.426
  421.5 1.6 copy.87
  423.1 1.3 mul.432
  424.5 0.5 copy.88
  425.0 1.3 mul.435
  426.3 1.3 add_multiply_fusion
  (90 shorter events, 2.0 us)
Async XLA Ops:
  0.7 2.7 copy-start
  129.9 2.4 copy-start.9
  160.6 15.3 %copy-start.10 = (bf16[2,256,768]{2,1,0:T(8,128)(2,1)S(1)}, bf16[2,256,768]{2,1,0:T(8,128)(2,1)}, u32[]{:S(2)}) copy-start(bf16[2,256,768]{2,1,0:T(8,128)(2,1)} %x_ref.1) | copy-start | bytes 2359300
  175.8 2.5 copy-start.3
  193.9 3.2 copy-start.5
  193.9 5.0 %copy-start.15 = (f32[512,3072]{1,0:T(8,128)S(1)}, f32[512,3072]{1,0:T(8,128)}, u32[]{:S(2)}) copy-start(f32[512,3072]{1,0:T(8,128)} %get-tuple-element.92) | copy-start | bytes 18874372
  197.1 8.6 %slice-start = ((s8[4718592]{0:T(1024)(128)(4,1)}), s8[4194304]{0:T(1024)(128)(4,1)S(1)}, s32[]{:S(2)}) async-start(s8[4718592]{0:T(1024)(128)(4,1)} %bitcast.106), calls=%async_computation | async-start | bytes 8388608
  198.9 6.9 %copy-start.6 = (f32[512,768]{1,0:T(8,128)}, f32[512,768]{1,0:T(8,128)S(1)}, u32[]{:S(2)}) copy-start(f32[512,768]{1,0:T(8,128)S(1)} %get-tuple-element.60) | copy-start | bytes 4718596
  198.9 6.9 %slice-start.1 = ((s8[4718592]{0:T(1024)(128)(4,1)}), s8[524288]{0:T(1024)(128)(4,1)S(1)}, s32[]{:S(2)}) async-start(s8[4718592]{0:T(1024)(128)(4,1)} %bitcast.106), calls=%async_computation.1 | async-start | bytes 1048576
  205.7 3.2 copy-start.16
  208.9 1.3 copy-start.14
  265.6 2.5 copy-start.13
  270.7 6.5 %copy-start.2 = (bf16[2,1024,576]{2,1,0:T(8,128)(2,1)S(1)}, bf16[2,1024,576]{2,1,0:T(8,128)(2,1)}, u32[]{:S(2)}) copy-start(bf16[2,1024,576]{2,1,0:T(8,128)(2,1)} %attend_back.1) | copy-start | bytes 7077892
  270.7 6.5 %copy-start.4 = (bf16[2,1024,768]{2,1,0:T(8,128)(2,1)S(1)}, bf16[2,1024,768]{2,1,0:T(8,128)(2,1)}, u32[]{:S(2)}) copy-start(bf16[2,1024,768]{2,1,0:T(8,128)(2,1)} %get-tuple-element.33.x_ref) | copy-start | bytes 9437188
  282.6 3.1 copy-start.7
  285.7 6.8 %copy-start.17 = (bf16[512,3072]{1,0:T(8,128)(2,1)S(1)}, bf16[512,3072]{1,0:T(8,128)(2,1)}, u32[]{:S(2)}) copy-start(bf16[512,3072]{1,0:T(8,128)(2,1)} %copy-done.16) | copy-start | bytes 9437188
  410.4 3.6 copy-start.8
  414.1 1.7 copy-start.12
  425.0 1.3 copy-start.11
  426.3 2.7 copy-start.1
